TPU v7x, 32 devices: a whole 2x2x4 slice. The times are simulated.
32 devices in a mesh: gx: 4 (over z), gy: 8 (over y, x, core).
Axes of the slice: x: 2, y: 2, z: 4, core: 2. Of those that a mesh axis runs over, the one named last changes fastest.
Arguments:
- right_side: float32 [512, 2048], P('gx', 'gy'), may hold values from -1.2 to 1.2
- shift: float32 [512, 2048], P('gx', 'gy'), may hold values from 0.0001 to 0.004
Outputs:
- solution: float32 [512, 2048], P('gx', 'gy')
- residual: float32 [512, 2048], P('gx', 'gy')
All inputs are finite; a program needn't handle non-finite values.
Results may differ from a plain program's by a relative error of at most 0.0003.
Values sent between devices are 32-bit elements; how exact they have to be, the bound alone decides.
A program may use at most 128 MiB of HBM per device.

v0:
```python
import jax
import jax.numpy as jnp
from jax import lax
from jax.sharding import PartitionSpec as P

LEVELS = 4
COARSE_SWEEPS = 6


damping = 0.8


def padded_2(cells, sides, width):
    for axis, dim in sides:
        count = lax.axis_size(axis)
        ends = count - 1
        head = lax.slice_in_dim(cells, 0, width, axis=dim)
        tail = lax.slice_in_dim(cells, cells.shape[dim] - width, cells.shape[dim], axis=dim)
        cells = jnp.concatenate(
            [
                lax.ppermute(tail, axis, [(i, (i + 1) % count) for i in range(ends)]),
                cells,
                lax.ppermute(head, axis, [((i + 1) % count, i) for i in range(ends)]),
            ],
            axis=dim,
        )
    return cells


def restrict(values):
    rows, columns = values.shape
    blocks = values.reshape(rows // 2, 2, columns // 2, 2)
    return 0.25 * (
        blocks[:, 0, :, 0] + blocks[:, 1, :, 0] + blocks[:, 0, :, 1] + blocks[:, 1, :, 1]
    )


def prolong(values):
    rows, columns = values.shape
    copies = jnp.broadcast_to(values[:, None, :, None], (rows, 2, columns, 2))
    return copies.reshape(2 * rows, 2 * columns)


def operate_padded(padded, shifts, level):
    centre = padded[1:-1, 1:-1]
    beside = padded[2:, 1:-1] + padded[:-2, 1:-1] + padded[1:-1, 2:] + padded[1:-1, :-2]
    return 4.0 ** (-level) * (4.0 * centre - beside) + shifts * centre


def with_rim(field):
    return padded_2(field, (("gx", 0), ("gy", 1)), 1)


def build_levels(shift):
    levels = []
    shifts = shift
    for level in range(LEVELS + 1):
        diagonal = 4.0 ** (1 - level) + shifts
        outer_shift = None
        inside = None
        levels.append((shifts, diagonal, outer_shift, inside))
        if level < LEVELS:
            shifts = restrict(shifts)
    return levels


def sweep_once(iterate, source, section, level):
    shifts, diagonal = (section[0], section[1])
    if iterate is None:
        return damping * source / diagonal
    return (
        iterate + damping * (source - operate_padded(with_rim(iterate), shifts, level)) / diagonal
    )


def smooth_two(iterate, source, section, level):
    iterate = sweep_once(iterate, source, section, level)
    return sweep_once(iterate, source, section, level)


def residual_of(iterate, source, section, level):
    return source - operate_padded(with_rim(iterate), section[0], level)


def gather_early(field):
    row_band = lax.all_gather(field, "gy", axis=1, tiled=True)
    return lax.all_gather(row_band, "gx", axis=0, tiled=True)


def local_sweeps(iterate, source, shifts, level, count):
    diagonal = 4.0 ** (1 - level) + shifts
    for turn in range(count):
        if iterate is None:
            iterate = damping * source / diagonal
        else:
            iterate = (
                iterate
                + damping * (source - operate_padded(jnp.pad(iterate, 1), shifts, level)) / diagonal
            )
    return iterate


def local_coarse(iterate, source, shifts):
    unit_total = jnp.sum(operate_padded(jnp.pad(jnp.ones_like(source), 1), shifts, LEVELS))
    if iterate is None:
        left = jnp.sum(source)
        iterate = jnp.zeros_like(source) + left / unit_total
    else:
        left = jnp.sum(source - operate_padded(jnp.pad(iterate, 1), shifts, LEVELS))
        iterate = iterate + left / unit_total
    return local_sweeps(iterate, source, shifts, LEVELS, COARSE_SWEEPS)


def local_vcycle(level, iterate, source, shift_table):
    shifts = shift_table[level]
    if level == LEVELS:
        return local_coarse(iterate, source, shifts)
    iterate = local_sweeps(iterate, source, shifts, level, 2)
    coarse_rhs = restrict(source - operate_padded(jnp.pad(iterate, 1), shifts, level))
    iterate = iterate + prolong(local_vcycle(level + 1, None, coarse_rhs, shift_table))
    return local_sweeps(iterate, source, shifts, level, 2)


def local_fcycle(level, source, shift_table):
    shifts = shift_table[level]
    if level == LEVELS:
        return local_coarse(None, source, shifts)
    iterate = local_sweeps(None, source, shifts, level, 2)
    coarse_rhs = restrict(source - operate_padded(jnp.pad(iterate, 1), shifts, level))
    correction = local_fcycle(level + 1, coarse_rhs, shift_table)
    correction = local_vcycle(level + 1, correction, coarse_rhs, shift_table)
    iterate = iterate + prolong(correction)
    return local_sweeps(iterate, source, shifts, level, 2)


def own_block(whole, rows, columns):
    return lax.dynamic_slice(
        whole, (lax.axis_index("gx") * rows, lax.axis_index("gy") * columns), (rows, columns)
    )


def early_solve(coarse_rhs, shift_table, full):
    whole_rhs = gather_early(coarse_rhs)
    if full:
        whole = local_fcycle(LEVELS - 1, whole_rhs, shift_table)
        whole = local_vcycle(LEVELS - 1, whole, whole_rhs, shift_table)
    else:
        whole = local_vcycle(LEVELS - 1, None, whole_rhs, shift_table)
    return own_block(whole, coarse_rhs.shape[0], coarse_rhs.shape[1])


def vcycle(level, iterate, source, levels, shift_whole):
    section = levels[level]
    iterate = smooth_two(iterate, source, section, level)
    coarse_rhs = restrict(residual_of(iterate, source, section, level))
    if level + 1 == LEVELS - 1:
        correction = early_solve(coarse_rhs, shift_whole, False)
    else:
        correction = vcycle(level + 1, None, coarse_rhs, levels, shift_whole)
    iterate = iterate + prolong(correction)
    return smooth_two(iterate, source, section, level)


def fcycle(level, source, levels, shift_whole):
    section = levels[level]
    iterate = smooth_two(None, source, section, level)
    coarse_rhs = restrict(residual_of(iterate, source, section, level))
    if level + 1 == LEVELS - 1:
        correction = early_solve(coarse_rhs, shift_whole, True)
    else:
        correction = fcycle(level + 1, coarse_rhs, levels, shift_whole)
        correction = vcycle(level + 1, correction, coarse_rhs, levels, shift_whole)
    iterate = iterate + prolong(correction)
    return smooth_two(iterate, source, section, level)


def body(right_side, shift):
    levels = build_levels(shift)
    upper = gather_early(levels[LEVELS - 1][0])
    shift_whole = {LEVELS - 1: upper, LEVELS: restrict(upper)}
    solution = fcycle(0, right_side, levels, shift_whole)
    residual = residual_of(solution, right_side, levels[0], 0)
    return (solution, residual)


def solution(mesh):
    in_specs = (P("gx", "gy"), P("gx", "gy"))
    out_specs = (P("gx", "gy"), P("gx", "gy"))
    return jax.shard_map(body, mesh=mesh, in_specs=in_specs, out_specs=out_specs, check_vma=False)
```

profile of v0, /device:TPU:28, one launch (start us, length us, event | category | flops | bytes accessed | tf_op | source)
XLA Modules:
  0.0 715.0 jit_solution(5198619085677997498)
XLA Ops:
  5.3 10.5 %reshape.185 = f32[64,2,128,2]{3,2,1,0:T(8,128)} reshape(f32[128,256]{1,0:T(8,128)} %param.3) | data formatting | bytes 262144 | tf_op jit(solution)/shard_map/reshape | solution.py:32
  20.4 8.0 %fusion.1 = f32[64,128]{1,0:T(8,128)S(1)} fusion(f32[64,2,128,2]{3,2,1,0:T(8,128)} %reshape.185), kind=kLoop, calls=%fused_computation.2 | loop fusion | flops 32768 | bytes 163840 | tf_op jit(solution)/shard_map/mul | solution.py:33
  50.5 9.8 %reshape.184 = f32[64,2,128,2]{3,2,1,0:T(8,128)} reshape(f32[128,256]{1,0:T(8,128)S(1)} %fusion.39) | data formatting | bytes 262144 | tf_op jit(solution)/shard_map/reshape | solution.py:32
  60.3 8.5 %multiply_reduce_fusion = (f32[64,128]{1,0:T(8,128)S(1)}, f32[64,128]{1,0:T(8,128)S(1)}) fusion(f32[64,2,128,2]{3,2,1,0:T(8,128)} %reshape.184), kind=kLoop, calls=%fused_computation.8 | loop fusion | flops 40960 | bytes 196608 | tf_op jit(solution)/shard_map/mul | solution.py:33
  72.8 14.8 %all-gather.2 = f32[16,1,256,1]{3,2,1,0:T(8,128)S(1)} all-gather(f32[16,1,32,1]{3,2,1,0:T(8,128)S(1)} %fusion.10), channel_id=4, replica_groups=mesh['gx'=4,'gy'=8] {'gy'}, dimensions={2}, use_global_device_ids=true | all-gather | bytes 18432 | tf_op jit(solution)/shard_map/all_gather | solution.py:86
  93.7 13.6 %all-gather.3 = f32[64,1,256,1]{2,3,1,0:T(1,128)S(1)} all-gather(f32[16,1,256,1]{2,3,1,0:T(1,128)S(1)} %copy.135), channel_id=5, replica_groups=mesh['gx'=4,'gy'=8] {'gx'}, dimensions={0}, use_global_device_ids=true | all-gather | bytes 81920 | tf_op jit(solution)/shard_map/all_gather | solution.py:87
  111.4 5.6 reshape.189
  128.6 4.5 collective-permute-start.16
  163.9 14.8 %all-gather = f32[16,1,256,1]{3,2,1,0:T(8,128)S(1)} all-gather(f32[16,1,32,1]{3,2,1,0:T(8,128)S(1)} %fusion.11), channel_id=2, replica_groups=mesh['gx'=4,'gy'=8] {'gy'}, dimensions={2}, use_global_device_ids=true | all-gather | bytes 18432 | tf_op jit(solution)/shard_map/all_gather | solution.py:86
  179.3 13.1 %all-gather.1 = f32[64,1,256,1]{2,3,1,0:T(1,128)S(1)} all-gather(f32[16,1,256,1]{2,3,1,0:T(1,128)S(1)} %copy.134), channel_id=3, replica_groups=mesh['gx'=4,'gy'=8] {'gx'}, dimensions={0}, use_global_device_ids=true | all-gather | bytes 81920 | tf_op jit(solution)/shard_map/all_gather | solution.py:87
  192.7 5.6 reshape.188
  198.3 8.6 %multiply_reduce_fusion.6 = (f32[32,128]{1,0:T(8,128)S(1)}, f32[32,1,128,1]{3,2,1,0:T(8,128)S(1)}, f32[]{:T(128)}, f32[32,128]{1,0:T(8,128)S(1)}) fusion(f32[32,2,128,2]{3,2,1,0:T(8,128)} %reshape.189, f32[32,2,128,2]{3,2,1,0:T(8,128)} %reshape.188), kind=kLoop, calls=%fused_computation.33 | loop fusion | flops 36863 | bytes 180228 | tf_op jit(solution)/shard_map/mul | solution.py:33
  220.0 5.6 reshape.191
  225.6 5.8 fusion.727
  241.3 10.9 %collective-permute-start.24 = (f32[1,64]{1,0:T(1,128)S(1)}, f32[1,64]{1,0:T(1,128)S(1)}, u32[]{:S(2)}, u32[]{:S(2)}) collective-permute-start(f32[1,64]{1,0:T(1,128)S(1)} %get-tuple-element.123), channel_id=1, source_target_pairs={{8,0},{16,8},{24,16},{9,1},{17,9},{25,17},{10,2},{18,10},{26,18},{... | collective-permute-start | bytes 776 | tf_op jit(solution)/shard_map/ppermute | solution.py:23
  331.4 15.1 %all-gather.4 = f32[16,1,256,1]{3,2,1,0:T(8,128)} all-gather(f32[16,1,32,1]{3,2,1,0:T(8,128)S(1)} %fusion.9), channel_id=6, replica_groups=mesh['gx'=4,'gy'=8] {'gy'}, dimensions={2}, use_global_device_ids=true | all-gather | bytes 18432 | tf_op jit(solution)/shard_map/all_gather | solution.py:86
  348.7 13.1 %all-gather.5 = f32[64,1,256,1]{2,3,1,0:T(1,128)S(1)} all-gather(f32[16,1,256,1]{2,3,1,0:T(1,128)S(1)} %copy.136), channel_id=7, replica_groups=mesh['gx'=4,'gy'=8] {'gx'}, dimensions={0}, use_global_device_ids=true | all-gather | bytes 81920 | tf_op jit(solution)/shard_map/all_gather | solution.py:87
  362.1 5.6 reshape.195
  367.7 5.8 fusion.726
  537.2 15.1 %all-gather.6 = f32[16,1,256,1]{3,2,1,0:T(8,128)} all-gather(f32[16,1,32,1]{3,2,1,0:T(8,128)S(1)} %fusion.8), channel_id=8, replica_groups=mesh['gx'=4,'gy'=8] {'gy'}, dimensions={2}, use_global_device_ids=true | all-gather | bytes 18432 | tf_op jit(solution)/shard_map/all_gather | solution.py:86
  554.5 13.1 %all-gather.7 = f32[64,1,256,1]{2,3,1,0:T(1,128)S(1)} all-gather(f32[16,1,256,1]{2,3,1,0:T(1,128)S(1)} %copy.137), channel_id=9, replica_groups=mesh['gx'=4,'gy'=8] {'gx'}, dimensions={0}, use_global_device_ids=true | all-gather | bytes 81920 | tf_op jit(solution)/shard_map/all_gather | solution.py:87
  567.9 5.6 reshape.201
  573.4 5.8 fusion.725
  658.5 6.9 reshape.205
  (449 shorter events, 478.9 us)
Async XLA Ops:
  1.6 14.2 %collective-permute-start = (f32[1,256]{1,0:T(1,128)S(1)}, f32[1,256]{1,0:T(1,128)S(1)}, u32[]{:S(2)}, u32[]{:S(2)}) collective-permute-start(f32[1,256]{1,0:T(1,128)S(1)} %get-tuple-element.37), channel_id=1, source_target_pairs={{8,0},{16,8},{24,16},{9,1},{17,9},{25,17},{10,2},{18,10},{26,18},{... | collective-permute-start | bytes 3080 | tf_op jit(solution)/shard_map/ppermute | solution.py:23
  4.0 11.8 %collective-permute-start.1 = (f32[1,256]{1,0:T(1,128)S(1)}, f32[1,256]{1,0:T(1,128)S(1)}, u32[]{:S(2)}, u32[]{:S(2)}) collective-permute-start(f32[1,256]{1,0:T(1,128)S(1)} %get-tuple-element.36), channel_id=1, source_target_pairs={{0,8},{8,16},{16,24},{1,9},{9,17},{17,25},{2,10},{10,18},{18,26},{... | collective-permute-start | bytes 3080 | tf_op jit(solution)/shard_map/ppermute | solution.py:21
  16.0 14.6 %collective-permute-start.2 = (f32[130,1]{1,0:T(8,128)S(1)}, f32[130,1]{1,0:T(8,128)S(1)}, u32[]{:S(2)}, u32[]{:S(2)}) collective-permute-start(f32[130,1]{1,0:T(8,128)S(1)} %get-tuple-element.26), channel_id=1, source_target_pairs={{1,0},{2,1},{3,2},{4,3},{5,4},{6,5},{7,6},{9,8},{10,9},{11,10},{12... | collective-permute-start | bytes 1568 | tf_op jit(solution)/shard_map/ppermute | solution.py:23
  18.5 12.1 %collective-permute-start.3 = (f32[130,1]{1,0:T(8,128)S(1)}, f32[130,1]{1,0:T(8,128)S(1)}, u32[]{:S(2)}, u32[]{:S(2)}) collective-permute-start(f32[130,1]{1,0:T(8,128)S(1)} %get-tuple-element.27), channel_id=1, source_target_pairs={{0,1},{1,2},{2,3},{3,4},{4,5},{5,6},{6,7},{8,9},{9,10},{10,11},{11... | collective-permute-start | bytes 1568 | tf_op jit(solution)/shard_map/ppermute | solution.py:21
  30.7 7.2 %collective-permute-start.4 = (f32[1,256]{1,0:T(1,128)S(1)}, f32[1,256]{1,0:T(1,128)S(1)}, u32[]{:S(2)}, u32[]{:S(2)}) collective-permute-start(f32[1,256]{1,0:T(1,128)S(1)} %get-tuple-element.35), channel_id=1, source_target_pairs={{8,0},{16,8},{24,16},{9,1},{17,9},{25,17},{10,2},{18,10},{26,18},{... | collective-permute-start | bytes 3080 | tf_op jit(solution)/shard_map/ppermute | solution.py:23
  43.8 6.5 collective-permute-start.7
  68.9 19.4 %collective-permute-start.8 = (f32[1,128]{1,0:T(1,128)S(1)}, f32[1,128]{1,0:T(1,128)S(1)}, u32[]{:S(2)}, u32[]{:S(2)}) collective-permute-start(f32[1,128]{1,0:T(1,128)S(1)} %get-tuple-element.75), channel_id=1, source_target_pairs={{8,0},{16,8},{24,16},{9,1},{17,9},{25,17},{10,2},{18,10},{26,18},{... | collective-permute-start | bytes 1544 | tf_op jit(solution)/shard_map/ppermute | solution.py:23
  71.5 16.8 %collective-permute-start.9 = (f32[1,128]{1,0:T(1,128)S(1)}, f32[1,128]{1,0:T(1,128)S(1)}, u32[]{:S(2)}, u32[]{:S(2)}) collective-permute-start(f32[1,128]{1,0:T(1,128)S(1)} %get-tuple-element.74), channel_id=1, source_target_pairs={{0,8},{8,16},{16,24},{1,9},{9,17},{17,25},{2,10},{10,18},{18,26},{... | collective-permute-start | bytes 1544 | tf_op jit(solution)/shard_map/ppermute | solution.py:21
  88.4 18.9 %collective-permute-start.10 = (f32[66,1]{1,0:T(8,128)S(1)}, f32[66,1]{1,0:T(8,128)S(1)}, u32[]{:S(2)}, u32[]{:S(2)}) collective-permute-start(f32[66,1]{1,0:T(8,128)S(1)} %get-tuple-element.56), channel_id=1, source_target_pairs={{1,0},{2,1},{3,2},{4,3},{5,4},{6,5},{7,6},{9,8},{10,9},{11,10},{12... | collective-permute-start | bytes 800 | tf_op jit(solution)/shard_map/ppermute | solution.py:23
  91.7 15.5 %collective-permute-start.11 = (f32[66,1]{1,0:T(8,128)S(1)}, f32[66,1]{1,0:T(8,128)S(1)}, u32[]{:S(2)}, u32[]{:S(2)}) collective-permute-start(f32[66,1]{1,0:T(8,128)S(1)} %get-tuple-element.57), channel_id=1, source_target_pairs={{0,1},{1,2},{2,3},{3,4},{4,5},{5,6},{6,7},{8,9},{9,10},{10,11},{11... | collective-permute-start | bytes 800 | tf_op jit(solution)/shard_map/ppermute | solution.py:21
  107.4 9.6 %collective-permute-start.12 = (f32[1,128]{1,0:T(1,128)S(1)}, f32[1,128]{1,0:T(1,128)S(1)}, u32[]{:S(2)}, u32[]{:S(2)}) collective-permute-start(f32[1,128]{1,0:T(1,128)S(1)} %get-tuple-element.73), channel_id=1, source_target_pairs={{8,0},{16,8},{24,16},{9,1},{17,9},{25,17},{10,2},{18,10},{26,18},{... | collective-permute-start | bytes 1544 | tf_op jit(solution)/shard_map/ppermute | solution.py:23
  110.0 7.0 collective-permute-start.13
  119.0 6.2 collective-permute-start.15
  241.3 12.2 %collective-permute-start.24 = (f32[1,64]{1,0:T(1,128)S(1)}, f32[1,64]{1,0:T(1,128)S(1)}, u32[]{:S(2)}, u32[]{:S(2)}) collective-permute-start(f32[1,64]{1,0:T(1,128)S(1)} %get-tuple-element.123), channel_id=1, source_target_pairs={{8,0},{16,8},{24,16},{9,1},{17,9},{25,17},{10,2},{18,10},{26,18},{... | collective-permute-start | bytes 776 | tf_op jit(solution)/shard_map/ppermute | solution.py:23
  429.3 6.2 collective-permute-start.55
  445.0 6.2 collective-permute-start.59
  460.9 6.2 collective-permute-start.63
  476.7 6.2 collective-permute-start.67
  492.4 6.2 collective-permute-start.71
  632.5 6.2 collective-permute-start.91
  648.2 6.2 collective-permute-start.95
  674.9 6.5 collective-permute-start.99
  691.0 6.5 collective-permute-start.103
  707.2 6.5 collective-permute-start.107
  (87 other events, 419.7 us)
where the time goes:
time: 727 us; the launch traced here: 715 us
  starting transfers between devices  227 us (31%)
  waiting for transfers between devices  192 us (26%)
  blocking collectives  113 us (16%)
  local copies, waits for them, and re-layouts  110 us (15%)
  other arithmetic  62.6 us (9%)
  between operations  10.1 us (1%)
    ppermute x54, waiting for transfers between devices, padded_2(): lax.ppermute(tail, axis, [(i, (i + 1) % count) for i in range(ends)])  191 us
    ppermute x54, starting transfers between devices, padded_2(): lax.ppermute(head, axis, [((i + 1) % count, i) for i in range(ends)])  129 us
    ppermute x54, starting transfers between devices, padded_2(): lax.ppermute(tail, axis, [(i, (i + 1) % count) for i in range(ends)])  98.4 us
    all_gather x4, blocking collectives, gather_early(): row_band = lax.all_gather(field, 'gy', axis=1, tiled=True)  59.9 us
    reshape x12, local copies, waits for them, and re-layouts, restrict(): blocks = values.reshape(rows // 2, 2, columns // 2, 2)  55.2 us
    all_gather x4, blocking collectives, gather_early(): return lax.all_gather(row_band, 'gx', axis=0, tiled=True)  53 us
    mul x13, other arithmetic, restrict(): 0.25 * (blocks[:, 0, :, 0] + blocks[:, 1, :, 0] + blocks[:, 0, :, 1] + bl...  48.9 us
    reshape x10, local copies, waits for them, and re-layouts, prolong(): return copies.reshape(2 * rows, 2 * columns)  27.8 us
  transfers between devices with their start and end apart: 108, of which 49 were waited for; matrix products, arithmetic and copies ran while one was open for 4% of the time, Pallas kernels for 0%

commit v1 on v0

v1 whole, which is shorter than its diff:
```python
import functools

import jax
import jax.numpy as jnp
from jax import lax
from jax.experimental import pallas as pl
from jax.experimental.pallas import tpu as pltpu
from jax.sharding import PartitionSpec as P

COARSE_SWEEPS = 6
DAMPING = 0.8
MESH = pl.DeviceIdType.MESH
F32 = jnp.float32
BF16 = jnp.bfloat16

ROWS_PAD = 8
HALO = 24


def iota(shape, dim):
    return lax.broadcasted_iota(jnp.int32, shape, dim)


def put_strips(ref, at, values):
    for k in range(ref.shape[0]):
        ref[k, at, :] = values[:, k * 128 : (k + 1) * 128]


def get_strips(ref, at, count=None):
    return jnp.concatenate([ref[k, at, :] for k in range(count or ref.shape[0])], 1)


def exact_dot(values, selector):
    first = values.astype(BF16)
    rest = values - first.astype(F32)
    second = rest.astype(BF16)
    third = (rest - second.astype(F32)).astype(BF16)
    dot = functools.partial(jnp.dot, preferred_element_type=F32)
    return dot(first, selector) + (dot(second, selector) + dot(third, selector))


def kernel(
    gx_count, gy_count, g_ref, s_ref, sol_ref, res_ref,
    gE, sE, wE, vA, vB, fine_add,
    g1, s1, w1, a1, b1, r1,
    send_l, send_r, recv_l, recv_r,
    down0, up0, down1, spread,
    rbuf, s2, w2, g2, a2, b2, s3, w3, g3, a3, b3, s4, w4, g4, a4, b4, picked,
    halo_send, halo_recv, all_send, all_recv,
):
    gx, gy = lax.axis_index("gx"), lax.axis_index("gy")
    total = gx_count * gy_count
    me = gx * gy_count + gy
    rows, cols = g_ref.shape
    base = ROWS_PAD + HALO
    base1 = ROWS_PAD + (ROWS_PAD + HALO) // 2
    ext, width = gE.shape
    ext1, width1 = ext // 2, g1.shape[1]
    lanes = 128

    zero_halo = jnp.zeros((base, width), F32)
    for ref in (gE, sE):
        ref[0:base, :] = zero_halo
        ref[base + rows : ext, :] = zero_halo
    for ref in (recv_l, recv_r):
        ref[...] = jnp.zeros(ref.shape, F32)
    barrier = pltpu.get_barrier_semaphore()

    @pl.loop(1, total)
    def _(k):
        peer = lax.rem(me + k, total)
        pl.semaphore_signal(
            barrier, inc=1, device_id=(peer // gy_count, lax.rem(peer, gy_count)), device_id_type=MESH
        )

    lane = iota((rows, lanes), 1)
    half = lanes // 2
    send_l[...] = jnp.where(lane < half, g_ref[:, 0:lanes], pltpu.roll(s_ref[:, 0:lanes], half, 1))
    send_r[...] = jnp.where(
        lane < half, pltpu.roll(s_ref[:, cols - lanes : cols], half, 1), g_ref[:, cols - lanes : cols]
    )

    l0 = iota((width, width1), 0)
    col0 = jnp.where(l0 < cols + half, l0, l0 - width)
    down0[...] = jnp.where(
        ((col0 + 2 * width1) // 2) % width1 == iota((width, width1), 1), 1.0, 0.0
    ).astype(BF16)
    l0 = iota((width1, width), 1)
    col0 = jnp.where(l0 < cols + half, l0, l0 - width)
    up0[...] = jnp.where(
        ((col0 + 2 * width1) // 2) % width1 == iota((width1, width), 0), 1.0, 0.0
    ).astype(BF16)
    l1 = iota((width1, lanes), 0)
    j2 = l1 // 2
    place = (j2 % 4) * 16 + j2 // 4
    down1[...] = jnp.where(
        (l1 < lanes) & (iota((width1, lanes), 1) % half == place), 1.0, 0.0
    ).astype(BF16)
    q_count = s2.shape[2]
    p_count = s2.shape[1]
    m1 = iota((q_count, width1), 1)
    col1 = jnp.where(m1 < lanes + half // 2, m1, m1 - width1)
    wide = gy * half + (col1 + 512) // 2 - 256
    for r in range(4):
        spread[r * q_count : (r + 1) * q_count, :] = jnp.where(
            wide == 4 * iota((q_count, width1), 0) + r, 1.0, 0.0
        ).astype(BF16)

    def pack_level2(source):
        parts = []
        for t in range(4):
            start = base1 + 2 * t
            parts.append(
                get_strips(source, pl.ds(start, 8, 8)) + get_strips(source, pl.ds(start + 1, 8, 8))
            )
        means = 0.25 * exact_dot(jnp.concatenate(parts, 0), down1[...])
        low = iota((16, lanes), 1) < half
        return jnp.where(low, means[0:16], means[16:32])

    half_rows = rows // 2
    own_strips = cols // lanes
    for k in range(own_strips):
        fine_add[k, base : base + rows, :] = s_ref[:, k * lanes : (k + 1) * lanes]
    own = get_strips(fine_add, pl.ds(base, half_rows, 2), own_strips)
    own = own + get_strips(fine_add, pl.ds(base + 1, half_rows, 2), own_strips)
    put_strips(r1, slice(base1, base1 + half_rows), 0.25 * exact_dot(own, down0[0:cols, :]))
    rbuf[0, me] = pack_level2(r1)
    gE[base : base + rows, 0:cols] = g_ref[...]
    sE[base : base + rows, 0:cols] = s_ref[...]

    pl.semaphore_wait(barrier, total - 1)

    top, bottom = slice(0, HALO), slice(rows - HALO, rows)
    above, below = slice(ROWS_PAD, base), slice(base + rows, base + rows + HALO)
    middle = slice(base, base + rows)
    sends = (
        (0, -1, send_l, recv_r.at[middle, :]),
        (0, 1, send_r, recv_l.at[middle, :]),
        (-1, -1, send_l.at[top, :], recv_r.at[below, :]),
        (1, -1, send_l.at[bottom, :], recv_r.at[above, :]),
        (-1, 1, send_r.at[top, :], recv_l.at[below, :]),
        (1, 1, send_r.at[bottom, :], recv_l.at[above, :]),
        (-1, 0, g_ref.at[top, :], gE.at[below, 0:cols]),
        (-1, 0, s_ref.at[top, :], sE.at[below, 0:cols]),
        (1, 0, g_ref.at[bottom, :], gE.at[above, 0:cols]),
        (1, 0, s_ref.at[bottom, :], sE.at[above, 0:cols]),
    )

    def inside(dx, dy):
        ok = None
        for step, at, count in ((dx, gx, gx_count), (dy, gy, gy_count)):
            if step:
                here = (at > 0) if step < 0 else (at < count - 1)
                ok = here if ok is None else ok & here
        return ok

    def halo_copy(n, dx, dy, source, target):
        return pltpu.make_async_remote_copy(
            src_ref=source, dst_ref=target, send_sem=halo_send.at[n], recv_sem=halo_recv.at[n],
            device_id=(gx + dx, gy + dy), device_id_type=MESH,
        )

    for n, (dx, dy, source, target) in enumerate(sends):
        @pl.when(inside(dx, dy))
        def _():
            halo_copy(n, dx, dy, source, target).start()

    def block_copy(turn, k, slot, peer):
        return pltpu.make_async_remote_copy(
            src_ref=rbuf.at[turn, me], dst_ref=rbuf.at[turn, slot],
            send_sem=all_send.at[turn, k], recv_sem=all_recv.at[turn, slot],
            device_id=(peer // gy_count, lax.rem(peer, gy_count)), device_id_type=MESH,
        )

    def gather_start(turn):
        @pl.loop(1, total)
        def _(k):
            block_copy(turn, k, me, lax.rem(me + k, total)).start()

    def gather_wait(turn):
        @pl.loop(1, total)
        def _(k):
            other = lax.rem(me + total - k, total)
            block_copy(turn, k, other, other).wait_recv()

    def gather_sent(turn):
        @pl.loop(1, total)
        def _(k):
            block_copy(turn, k, me, lax.rem(me + k, total)).wait_send()

    gather_start(0)
    zero_tile = jnp.zeros((ROWS_PAD, width), F32)
    for ref in (vA, vB):
        ref[0:ROWS_PAD, :] = zero_tile
        ref[ext - ROWS_PAD : ext, :] = zero_tile
    for ref in (a1, b1, g1):
        ref[0:ROWS_PAD, :] = jnp.zeros((ROWS_PAD, width1), F32)
        ref[ROWS_PAD + ext1 : 2 * ROWS_PAD + ext1, :] = jnp.zeros((ROWS_PAD, width1), F32)
    for ref in (a2, b2, a3, b3, a4, b4):
        for i in range(ref.shape[0]):
            ref[i, 0:8, :] = jnp.zeros((8, q_count), F32)
            ref[i, 8 + p_count : 16 + p_count, :] = jnp.zeros((8, q_count), F32)

    for n, (dx, dy, source, target) in enumerate(sends):
        @pl.when(inside(-dx, -dy))
        def _():
            halo_copy(n, -dx, -dy, source, target).wait_recv()

    lane_e = iota((ext, lanes), 1)
    gE[:, cols:width] = jnp.where(lane_e < half, recv_r[...], recv_l[...])
    sE[:, cols:width] = pltpu.roll(jnp.where(lane_e < half, recv_l[...], recv_r[...]), half, 1)

    def weight(shifts, first_row, own_rows, own_cols, split, level):
        shape = shifts.shape
        at_row = gx * own_rows + iota(shape, 0) + first_row
        lane_at = iota(shape, 1)
        at_col = gy * own_cols + jnp.where(lane_at < own_cols + split, lane_at, lane_at - shape[1])
        good = (at_row >= 0) & (at_row < gx_count * own_rows)
        good = good & (at_col >= 0) & (at_col < gy_count * own_cols)
        return jnp.where(good, DAMPING / (4.0 ** (1 - level) + shifts), 0.0)

    def around(v, lo, size):
        span = v.shape[1]
        mid = v[lo : lo + size, :]
        beside = pltpu.roll(mid, 1, 1) + pltpu.roll(mid, span - 1, 1)
        return mid, beside + (v[lo - 1 : lo - 1 + size, :] + v[lo + 1 : lo + 1 + size, :])

    def sweep_block(v, out, g, w, level):
        scale = 4.0 ** (-level)
        for lo in range(ROWS_PAD, v.shape[0] - ROWS_PAD, 8):
            mid, beside = around(v, lo, 8)
            at = slice(lo, lo + 8)
            out[at, :] = (1.0 - DAMPING) * mid + w[at, :] * (g[at, :] + scale * beside)

    def residual_block(v, out, g, s, level):
        scale = 4.0 ** (-level)
        for lo in range(ROWS_PAD, v.shape[0] - ROWS_PAD, 8):
            mid, beside = around(v, lo, 8)
            at = slice(lo, lo + 8)
            put_strips(out, at, g[at, :] - (scale * (4.0 * mid - beside) + s[at, :] * mid))

    chunk = 16
    for lo in range(0, ext, chunk):
        at = slice(lo, lo + chunk)
        wE[at, :] = weight(sE[at, :], lo - base, rows, cols, half, 0)
    for lo in range(ROWS_PAD, ext - ROWS_PAD, 8):
        at = slice(lo, lo + 8)
        vA[at, :] = wE[at, :] * gE[at, :]
    sweep_block(vA, vB, gE, wE, 0)
    put_strips(fine_add, slice(0, ROWS_PAD), zero_tile)
    put_strips(fine_add, slice(ext - ROWS_PAD, ext), zero_tile)
    residual_block(vB, fine_add, gE, sE, 0)

    in1 = slice(ROWS_PAD, ROWS_PAD + ext1)

    def halved():
        pairs = get_strips(fine_add, pl.ds(0, ext1, 2)) + get_strips(fine_add, pl.ds(1, ext1, 2))
        return 0.25 * exact_dot(pairs, down0[...])

    g1[in1, :] = halved()
    put_strips(fine_add, slice(0, ext), sE[...])
    s1[in1, :] = halved()
    w1[in1, :] = weight(s1[in1, :], ROWS_PAD - base1, half_rows, cols // 2, half // 2, 1)
    a1[in1, :] = w1[in1, :] * g1[in1, :]
    sweep_block(a1, b1, g1, w1, 1)
    residual_block(b1, r1, g1, s1, 1)
    rbuf[1, me] = pack_level2(r1)
    gather_start(1)

    block = (lane_e[0:8] // 16)

    def unpack(turn, target):
        for x in range(gx_count):
            for u in range(gy_count // 8):
                for tl in range(2):
                    tiles = [rbuf[turn, x * gy_count + u * 8 + g, tl * 8 : tl * 8 + 8, :] for g in range(8)]
                    for bit in (1, 2, 4):
                        keep = (block & bit) == 0
                        fresh = list(tiles)
                        for g in range(8):
                            if g & bit == 0:
                                lo, hi = tiles[g], tiles[g | bit]
                                fresh[g] = jnp.where(keep, lo, pltpu.roll(hi, 16 * bit, 1))
                                fresh[g | bit] = jnp.where(keep, pltpu.roll(lo, lanes - 16 * bit, 1), hi)
                        tiles = fresh
                    for b in range(8):
                        t, r = (b // 4) * 2 + tl, b % 4
                        target[t * 4 + r, 8 * x : 8 * x + 8, u * lanes : (u + 1) * lanes] = tiles[b]

    lane_q = iota((p_count, q_count), 1)
    rows_q = slice(8, 8 + p_count)

    def sides(v, n, t, r):
        mid = v[t * n + r, rows_q, :]
        if t > 0:
            north = v[(t - 1) * n + r, rows_q, :]
        else:
            north = v[(n - 1) * n + r, 7 : 7 + p_count, :]
        if t < n - 1:
            south = v[(t + 1) * n + r, rows_q, :]
        else:
            south = v[r, 9 : 9 + p_count, :]
        if r > 0:
            west = v[t * n + r - 1, rows_q, :]
        else:
            west = jnp.where(lane_q == 0, 0.0, pltpu.roll(v[t * n + n - 1, rows_q, :], 1, 1))
        if r < n - 1:
            east = v[t * n + r + 1, rows_q, :]
        else:
            east = jnp.where(
                lane_q == q_count - 1, 0.0, pltpu.roll(v[t * n, rows_q, :], q_count - 1, 1)
            )
        return mid, (north + south) + (west + east)

    level_refs = {2: (s2, w2, g2, a2, b2, 4), 3: (s3, w3, g3, a3, b3, 2), 4: (s4, w4, g4, a4, b4, 1)}

    def sweep(level, v, out):
        s, w, g, _, _, n = level_refs[level]
        for t in range(n):
            for r in range(n):
                i = t * n + r
                mid, beside = sides(v, n, t, r)
                out[i, rows_q, :] = (1.0 - DAMPING) * mid + w[i] * (g[i] + 4.0 ** (-level) * beside)

    def first_sweep(level, out):
        s, w, g, _, _, n = level_refs[level]
        for i in range(n * n):
            out[i, rows_q, :] = w[i] * g[i]

    def restricted(level, v):
        s, w, g, _, _, n = level_refs[level]
        coarse_g = level_refs[level + 1][2]
        for t in range(n // 2):
            for r in range(n // 2):
                sums = None
                for dt in range(2):
                    for dr in range(2):
                        i = (2 * t + dt) * n + 2 * r + dr
                        mid, beside = sides(v, n, 2 * t + dt, 2 * r + dr)
                        left = g[i] - (4.0 ** (-level) * (4.0 * mid - beside) + s[i] * mid)
                        sums = left if sums is None else sums + left
                coarse_g[t * (n // 2) + r] = 0.25 * sums

    def correct(level, v, e):
        n = level_refs[level][5]
        for t in range(n):
            for r in range(n):
                i = t * n + r
                v[i, rows_q, :] = v[i, rows_q, :] + e[(t // 2) * (n // 2) + r // 2, rows_q, :]

    def prepare(level):
        s, w, _, _, _, n = level_refs[level]
        for i in range(n * n):
            w[i] = DAMPING / (4.0 ** (1 - level) + s[i])
        if level < 4:
            coarse_s = level_refs[level + 1][0]
            m = n // 2
            for t in range(m):
                for r in range(m):
                    i = 2 * t * n + 2 * r
                    coarse_s[t * m + r] = 0.25 * ((s[i] + s[i + n]) + (s[i + 1] + s[i + n + 1]))

    def total_of(x):
        return jnp.sum(jnp.sum(x, axis=0, keepdims=True), axis=1, keepdims=True)

    gather_wait(0)
    unpack(0, s2)
    for level in (2, 3, 4):
        prepare(level)
    row_q = iota((p_count, q_count), 0)
    edges = jnp.where(row_q == 0, 1.0, 0.0) + jnp.where(row_q == p_count - 1, 1.0, 0.0)
    edges = edges + jnp.where(lane_q == 0, 1.0, 0.0) + jnp.where(lane_q == q_count - 1, 1.0, 0.0)
    per_unit = 1.0 / total_of(4.0 ** (-4) * edges + s4[0])

    def coarse(v, from_zero):
        if from_zero:
            shifted = jnp.zeros((p_count, q_count), F32) + total_of(g4[0]) * per_unit
        else:
            mid, beside = sides(v, 1, 0, 0)
            left = g4[0] - (4.0 ** (-4) * (4.0 * mid - beside) + s4[0] * mid)
            shifted = mid + total_of(left) * per_unit
        now, later = a4, b4
        now[0, rows_q, :] = shifted
        for _ in range(COARSE_SWEEPS):
            sweep(4, now, later)
            now, later = later, now
        return now

    def vcycle(level, v):
        if level == 4:
            return coarse(v, v is None)
        _, _, _, a, b, n = level_refs[level]
        if v is None:
            first_sweep(level, a)
            sweep(level, a, b)
            now, later = b, a
        else:
            later = b if v is a else a
            sweep(level, v, later)
            sweep(level, later, v)
            now = v
        restricted(level, now)
        correct(level, now, vcycle(level + 1, None))
        sweep(level, now, later)
        sweep(level, later, now)
        return now

    def fcycle(level):
        if level == 4:
            return coarse(None, True)
        _, _, _, a, b, n = level_refs[level]
        first_sweep(level, a)
        sweep(level, a, b)
        restricted(level, b)
        e = fcycle(level + 1)
        e = vcycle(level + 1, e)
        correct(level, b, e)
        sweep(level, b, a)
        sweep(level, a, b)
        return b

    def add_level2(e, v):
        for t in range(4):
            tiles = [e[t * 4 + r, pl.ds(pl.multiple_of(gx * 8, 8), 24), :] for r in range(4)]
            picked[t] = exact_dot(jnp.concatenate(tiles, 1), spread[...])
        for t in range(4):
            for a in range(2):
                at = pl.ds(ROWS_PAD + 2 * t + a, ext1 // 8, 8)
                put_strips(r1, at, picked[t, 6 : 6 + ext1 // 8, :])
        v[in1, :] = v[in1, :] + get_strips(r1, in1)

    gather_wait(1)
    unpack(1, g2)
    e = fcycle(2)
    e = vcycle(2, e)
    add_level2(e, b1)
    sweep_block(b1, a1, g1, w1, 1)
    sweep_block(a1, b1, g1, w1, 1)
    sweep_block(b1, a1, g1, w1, 1)
    sweep_block(a1, b1, g1, w1, 1)
    residual_block(b1, r1, g1, s1, 1)
    rbuf[2, me] = pack_level2(r1)
    gather_start(2)
    gather_wait(2)
    unpack(2, g2)
    add_level2(vcycle(2, None), b1)
    sweep_block(b1, a1, g1, w1, 1)
    sweep_block(a1, b1, g1, w1, 1)
    raised = exact_dot(b1[in1, :], up0[...])
    put_strips(fine_add, pl.ds(0, ext1, 2), raised)
    put_strips(fine_add, pl.ds(1, ext1, 2), raised)
    for lo in range(ROWS_PAD, ext - ROWS_PAD, 8):
        at = slice(lo, lo + 8)
        vB[at, :] = vB[at, :] + get_strips(fine_add, at)
    sweep_block(vB, vA, gE, wE, 0)
    sweep_block(vA, vB, gE, wE, 0)
    for lo in range(0, rows, 8):
        mid, beside = around(vB, base + lo, 8)
        at = slice(base + lo, base + lo + 8)
        left = gE[at, :] - ((4.0 * mid - beside) + sE[at, :] * mid)
        sol_ref[lo : lo + 8, :] = mid[:, 0:cols]
        res_ref[lo : lo + 8, :] = left[:, 0:cols]

    for n, (dx, dy, source, target) in enumerate(sends):
        @pl.when(inside(dx, dy))
        def _():
            halo_copy(n, dx, dy, source, target).wait_send()
    for turn in range(3):
        gather_sent(turn)


def solution(mesh):
    gx_count, gy_count = mesh.shape["gx"], mesh.shape["gy"]
    total = gx_count * gy_count

    def body(right_side, shift):
        rows, cols = right_side.shape
        assert cols == 256 and rows % 64 == 0 and gy_count % 8 == 0
        ext, width = rows + 2 * (HALO + ROWS_PAD), cols + 128
        ext1, width1 = ext // 2 + 2 * ROWS_PAD, 256
        p, q = rows // 16 * gx_count, cols // 16 * gy_count
        V = pltpu.VMEM
        big = [V((ext, width), F32)] * 5 + [V((width // 128, ext, 128), F32)]
        one = [V((ext1, width1), F32)] * 5 + [V((width1 // 128, ext1, 128), F32)]
        levels = []
        for n in (16, 4, 1):
            levels += [V((n, p, q), F32)] * 3 + [V((n, p + 16, q), F32)] * 2
        scratch = (
            big + one
            + [V((rows, 128), F32)] * 2 + [V((ext, 128), F32)] * 2
            + [V((width, width1), BF16), V((width1, width), BF16), V((width1, 128), BF16), V((4 * q, width1), BF16)]
            + [V((3, total, 16, 128), F32)]
            + levels
            + [V((4, 24, width1), F32)]
            + [
                pltpu.SemaphoreType.DMA((10,)), pltpu.SemaphoreType.DMA((10,)),
                pltpu.SemaphoreType.DMA((3, total)), pltpu.SemaphoreType.DMA((3, total)),
            ]
        )
        out = jax.ShapeDtypeStruct(right_side.shape, F32)
        return pl.pallas_call(
            functools.partial(kernel, gx_count, gy_count),
            out_shape=(out, out),
            in_specs=[pl.BlockSpec(memory_space=pltpu.VMEM)] * 2,
            out_specs=(pl.BlockSpec(memory_space=pltpu.VMEM),) * 2,
            scratch_shapes=scratch,
            compiler_params=pltpu.CompilerParams(
                collective_id=0, has_side_effects=True, vmem_limit_bytes=60 * 1024 * 1024
            ),
        )(right_side, shift)

    spec = P("gx", "gy")
    return jax.shard_map(body, mesh=mesh, in_specs=(spec, spec), out_specs=(spec, spec), check_vma=False)
```

time: 727 us -> 43.7 us (0.06)
  the two profiles are of different devices: /device:TPU:28 before, /device:TPU:0 now
where the time goes in v1:
time: 43.7 us; the launch traced here: 43.6 us
  Pallas kernels  40.6 us (93%)
  local copies, waits for them, and re-layouts  2.26 us (5%)
  between operations  0.65 us (1%)
    pallas_call x1, Pallas kernels, body(): pl.pallas_call(functools.partial(kernel, gx_count, gy_count), out_shape=(...  40.6 us
    unnamed x4, local copies, waits for them, and re-layouts  2.26 us

profile of v1, /device:TPU:0, one launch (start us, length us, event | category | flops | bytes accessed | tf_op | source)
XLA Modules:
  0.0 43.6 jit_solution(15161352092291931775)
XLA Ops:
  0.6 40.6 %shard_map.41 = (f32[128,256]{1,0:T(8,128)}, f32[128,256]{1,0:T(8,128)}) custom-call(f32[128,256]{1,0:T(8,128)} %g_ref.1, f32[128,256]{1,0:T(8,128)} %s_ref.1), custom_call_target="tpu_custom_call" | custom-call | tf_op jit(solution)/shard_map/pallas_call | solution.py:501
  41.3 0.0 copy-start
  41.3 1.6 %copy.6 = f32[128,256]{1,0:T(8,128)} copy(f32[128,256]{1,0:T(8,128)} %get-tuple-element.4) | data formatting | bytes 262144
  42.9 0.0 copy-done
  42.9 0.7 %copy.7 = f32[128,256]{1,0:T(8,128)} copy(f32[128,256]{1,0:T(8,128)S(1)} %copy-done) | data formatting | bytes 262144
Async XLA Ops:
  41.3 1.6 %copy-start = (f32[128,256]{1,0:T(8,128)S(1)}, f32[128,256]{1,0:T(8,128)}, u32[]{:S(2)}) copy-start(f32[128,256]{1,0:T(8,128)} %get-tuple-element.5) | copy-start | bytes 393220

commit v2 on v1

--- a/solution.py
+++ b/solution.py
@@ -40,7 +40,7 @@
 
 
 def kernel(
-    gx_count, gy_count, g_ref, s_ref, sol_ref, res_ref,
+    gx_count, gy_count, g_ref, s_ref, out_ref,
     gE, sE, wE, vA, vB, fine_add,
     g1, s1, w1, a1, b1, r1,
     send_l, send_r, recv_l, recv_r,
@@ -165,28 +165,59 @@
         def _():
             halo_copy(n, dx, dy, source, target).start()
 
-    def block_copy(turn, k, slot, peer):
+    core = lax.rem(gy, 2)
+    per_row = gy_count // 2
+    chips = total // 2
+    chip = me // 2
+    partner = (gx, gy + 1 - 2 * core)
+
+    def zigzag(j):
+        odd = lax.rem(j, 2)
+        return odd * ((j + 1) // 2) + (1 - odd) * (chips - j // 2)
+
+    def block_copy(turn, n, slot, peer):
         return pltpu.make_async_remote_copy(
-            src_ref=rbuf.at[turn, me], dst_ref=rbuf.at[turn, slot],
-            send_sem=all_send.at[turn, k], recv_sem=all_recv.at[turn, slot],
-            device_id=(peer // gy_count, lax.rem(peer, gy_count)), device_id_type=MESH,
+            src_ref=rbuf.at[turn, slot], dst_ref=rbuf.at[turn, slot],
+            send_sem=all_send.at[turn, n], recv_sem=all_recv.at[turn, slot],
+            device_id=peer, device_id_type=MESH,
         )
 
+    def direct(turn, j):
+        other = lax.rem(chip + zigzag(j), chips)
+        return block_copy(turn, j, me, (other // per_row, 2 * lax.rem(other, per_row) + core))
+
+    def onward(turn, j):
+        slot = 2 * lax.rem(chip + chips - zigzag(j), chips) + core
+        return block_copy(turn, chips + j, slot, partner)
+
     def gather_start(turn):
-        @pl.loop(1, total)
-        def _(k):
-            block_copy(turn, k, me, lax.rem(me + k, total)).start()
+        block_copy(turn, 0, me, partner).start()
+
+        @pl.loop(1, chips)
+        def _(j):
+            direct(turn, chips - j).start()
 
     def gather_wait(turn):
-        @pl.loop(1, total)
-        def _(k):
-            other = lax.rem(me + total - k, total)
-            block_copy(turn, k, other, other).wait_recv()
+        @pl.loop(1, chips)
+        def _(j):
+            copy = onward(turn, j)
+            copy.wait_recv()
+            copy.start()
+
+        block_copy(turn, 0, me + 1 - 2 * core, partner).wait_recv()
+
+        @pl.loop(1, chips)
+        def _(j):
+            slot = 2 * lax.rem(chip + chips - zigzag(j), chips) + 1 - core
+            block_copy(turn, chips + j, slot, partner).wait_recv()
 
     def gather_sent(turn):
-        @pl.loop(1, total)
-        def _(k):
-            block_copy(turn, k, me, lax.rem(me + k, total)).wait_send()
+        block_copy(turn, 0, me, partner).wait_send()
+
+        @pl.loop(1, chips)
+        def _(j):
+            direct(turn, j).wait_send()
+            onward(turn, j).wait_send()
 
     gather_start(0)
     zero_tile = jnp.zeros((ROWS_PAD, width), F32)
@@ -458,8 +489,8 @@
         mid, beside = around(vB, base + lo, 8)
         at = slice(base + lo, base + lo + 8)
         left = gE[at, :] - ((4.0 * mid - beside) + sE[at, :] * mid)
-        sol_ref[lo : lo + 8, :] = mid[:, 0:cols]
-        res_ref[lo : lo + 8, :] = left[:, 0:cols]
+        out_ref[0, lo : lo + 8, :] = mid[:, 0:cols]
+        out_ref[1, lo : lo + 8, :] = left[:, 0:cols]
 
     for n, (dx, dy, source, target) in enumerate(sends):
         @pl.when(inside(dx, dy))
@@ -497,17 +528,18 @@
                 pltpu.SemaphoreType.DMA((3, total)), pltpu.SemaphoreType.DMA((3, total)),
             ]
         )
-        out = jax.ShapeDtypeStruct(right_side.shape, F32)
-        return pl.pallas_call(
+        out = jax.ShapeDtypeStruct((2,) + right_side.shape, F32)
+        both = pl.pallas_call(
             functools.partial(kernel, gx_count, gy_count),
-            out_shape=(out, out),
+            out_shape=out,
             in_specs=[pl.BlockSpec(memory_space=pltpu.VMEM)] * 2,
-            out_specs=(pl.BlockSpec(memory_space=pltpu.VMEM),) * 2,
+            out_specs=pl.BlockSpec(memory_space=pltpu.VMEM),
             scratch_shapes=scratch,
             compiler_params=pltpu.CompilerParams(
                 collective_id=0, has_side_effects=True, vmem_limit_bytes=60 * 1024 * 1024
             ),
         )(right_side, shift)
+        return both[0], both[1]
 
     spec = P("gx", "gy")
     return jax.shard_map(body, mesh=mesh, in_specs=(spec, spec), out_specs=(spec, spec), check_vma=False)

time: 43.7 us -> 41.2 us (0.943)
  Pallas kernels: 40.6 us -> 38.4 us
  local copies, waits for them, and re-layouts: 2.26 us -> 1.69 us
    unnamed x4 -> x0, local copies, waits for them, and re-layouts: 2.26 us -> none
    pallas_call x1, Pallas kernels: 40.6 us -> 38.4 us  [body(): pl.pallas_call(functools.partial(kernel, gx_count, gy_count), out_shape=o...]
    squeeze x0 -> x1, local copies, waits for them, and re-layouts: none -> 1.69 us  [body(): return (both[0], both[1])]
where the time goes in v2:
time: 41.2 us; the launch traced here: 40.7 us
  Pallas kernels  38.4 us (93%)
  local copies, waits for them, and re-layouts  1.69 us (4%)
  between operations  0.64 us (2%)
    pallas_call x1, Pallas kernels, body(): pl.pallas_call(functools.partial(kernel, gx_count, gy_count), out_shape=o...  38.4 us
    squeeze x1, local copies, waits for them, and re-layouts, body(): return (both[0], both[1])  1.69 us

profile of v2, /device:TPU:0, one launch (start us, length us, event | category | flops | bytes accessed | tf_op | source)
XLA Modules:
  0.0 40.7 jit_solution(11593720650936204425)
XLA Ops:
  0.6 38.4 %shard_map.41 = f32[2,128,256]{2,1,0:T(8,128)} custom-call(f32[128,256]{1,0:T(8,128)} %g_ref.1, f32[128,256]{1,0:T(8,128)} %s_ref.1), custom_call_target="tpu_custom_call" | custom-call | tf_op jit(solution)/shard_map/pallas_call | solution.py:532
  39.0 1.7 %slice_bitcast_fusion = (f32[128,256]{1,0:T(8,128)}, f32[128,256]{1,0:T(8,128)}) fusion(f32[2,128,256]{2,1,0:T(8,128)} %shard_map.41), kind=kLoop, calls=%fused_computation | loop fusion | bytes 524288 | tf_op jit(solution)/shard_map/squeeze | solution.py:542
